TPU v7x, 256 devices: a whole 4x4x8 slice. The times are simulated.
256 devices in a mesh: expert: 128 (over y, x, z), dp: 2 (over core).
Axes of the slice: x: 4, y: 4, z: 8, core: 2. Of those that a mesh axis runs over, the one named last changes fastest.
Arguments:
- tokens: bfloat16 [4096, 2048], P(('dp', 'expert')), parts along dimension 0, may hold values from -6 to 6
- expert_ids: int32 [4096, 8], P(('dp', 'expert')), parts along dimension 0, may hold values from 0 to 127, all different within a row; in each aligned block of 16 rows (0 to 15, 16 to 31, ...) at most 2 rows name the same one
- gate_values: float32 [4096, 8], P(('dp', 'expert')), parts along dimension 0, may hold values from 0.03 to 0.4
- w_gate: bfloat16 [128, 2048, 768], P('expert'), may hold values from -0.125 to 0.125
- w_up: bfloat16 [128, 2048, 768], P('expert'), may hold values from -0.125 to 0.125
- w_down: bfloat16 [128, 768, 2048], P('expert'), may hold values from -0.21875 to 0.21875
- cotangent: bfloat16 [4096, 2048], P(('dp', 'expert')), parts along dimension 0, may hold values from -6 to 6
Outputs:
- mixed_rows: bfloat16 [4096, 2048], P(('dp', 'expert')), parts along dimension 0
- row_grads: bfloat16 [4096, 2048], P(('dp', 'expert')), parts along dimension 0
- gate_grads: float32 [4096, 8], P(('dp', 'expert')), parts along dimension 0
There are 2 independent parts, one for each index of `dp`. A program takes and returns all parts, laid end to end along the dimension named above; an argument that names none is the same for every part. Nothing has to cross between parts.
Inputs may be any that keep to these rules, and one draw needn't show every extreme that they name: `expert_ids`: each token names 8 different experts. Among the 16 tokens of one device no expert is named more than 2 times, and in every draw some device names some expert exactly 2 times.
All inputs are finite; a program needn't handle non-finite values.
Results may differ from a plain program's by a relative error of at most 0.0064.
Values may be sent and summed in bfloat16 or wider, within the bound.
No kernel may reach another device: no remote copies, remote signals or barrier semaphores. Data moves between devices by JAX's collectives and lax.ppermute only.
A program may use at most 128 MiB of HBM per device.

v0:
```python
import jax
import jax.numpy as jnp
from jax import lax
from jax.sharding import PartitionSpec as P


def expert_forward(inputs, gate_matrix, up_matrix, down_matrix):
    pre_gate = jnp.dot(inputs, gate_matrix, preferred_element_type=jnp.float32)
    pre_up = jnp.dot(inputs, up_matrix, preferred_element_type=jnp.float32)
    hidden = (pre_gate * jax.nn.sigmoid(pre_gate) * pre_up).astype(jnp.bfloat16)
    output = jnp.dot(hidden, down_matrix, preferred_element_type=jnp.float32).astype(jnp.bfloat16)
    return (output, pre_gate, pre_up)


def expert_backward(grad_output, pre_gate, pre_up, gate_matrix, up_matrix, down_matrix):
    contract = (((1,), (1,)), ((), ()))
    grad_hidden = lax.dot_general(
        grad_output, down_matrix, contract, preferred_element_type=jnp.float32
    )
    sigmoid = jax.nn.sigmoid(pre_gate)
    grad_gate = (grad_hidden * pre_up * sigmoid * (1.0 + pre_gate * (1.0 - sigmoid))).astype(
        jnp.bfloat16
    )
    grad_up = (grad_hidden * pre_gate * sigmoid).astype(jnp.bfloat16)
    first_part = lax.dot_general(
        grad_gate, gate_matrix, contract, preferred_element_type=jnp.float32
    )
    second_part = lax.dot_general(grad_up, up_matrix, contract, preferred_element_type=jnp.float32)
    return (first_part + second_part).astype(jnp.bfloat16)


def slot_places(expert_ids, experts, capacity):
    flat_ids = expert_ids.reshape(-1)
    matches = (flat_ids[:, None] == jnp.arange(experts, dtype=jnp.int32)[None, :]).astype(jnp.int32)
    ranked = jnp.sum((jnp.cumsum(matches, axis=0) - matches) * matches, axis=1)
    return flat_ids * capacity + ranked


def local(tokens, expert_ids, gate_values, w_gate, w_up, w_down, cotangent):
    row_count, model_width = tokens.shape
    top_count = expert_ids.shape[1]
    experts = lax.axis_size("expert")
    capacity = max(2, 2 * row_count * top_count // experts)
    slot_total = experts * capacity
    entry_count = row_count * top_count
    gate_matrix = w_gate[0]
    up_matrix = w_up[0]
    down_matrix = w_down[0]
    places = slot_places(expert_ids, experts, capacity)
    flat_gates = gate_values.reshape(-1)
    upstream = jnp.repeat(cotangent, top_count, axis=0)
    padding = jnp.zeros((1, model_width), jnp.bfloat16)
    gathered_ids = lax.all_gather(expert_ids, "expert", axis=0, tiled=True)
    all_gates = lax.all_gather(gate_values, "expert", axis=0, tiled=True)
    all_tokens, all_cotangent = (
        lax.all_gather(tokens, "expert", axis=0, tiled=True),
        lax.all_gather(cotangent, "expert", axis=0, tiled=True),
    )
    own_expert = lax.axis_index("expert")
    all_flat = gathered_ids.reshape(experts, entry_count)
    matches = (all_flat == own_expert).astype(jnp.int32)
    ranked = jnp.cumsum(matches, axis=1) - matches
    sources = jnp.arange(experts, dtype=jnp.int32)[:, None]
    placed = jnp.where(matches == 1, sources * capacity + ranked, slot_total)
    entries = sources * entry_count + jnp.arange(entry_count, dtype=jnp.int32)[None, :]
    slot_table = (
        jnp.full((slot_total + 1,), experts * entry_count, jnp.int32)
        .at[placed.reshape(-1)]
        .set(entries.reshape(-1))[:slot_total]
    )
    token_of = slot_table // top_count
    received = jnp.concatenate([all_tokens, padding], axis=0)[token_of]
    output, pre_gate, pre_up = expert_forward(received, gate_matrix, up_matrix, down_matrix)
    slot_gates = jnp.concatenate([all_gates.reshape(-1), jnp.zeros((1,), jnp.float32)])[slot_table]
    chosen = jnp.concatenate([all_cotangent, padding], axis=0)[token_of]
    incoming = (slot_gates[:, None] * chosen.astype(jnp.float32)).astype(jnp.bfloat16)
    grad_rows = expert_backward(incoming, pre_gate, pre_up, gate_matrix, up_matrix, down_matrix)
    returned = lax.all_to_all(
        output.reshape(experts, capacity, model_width),
        "expert",
        split_axis=0,
        concat_axis=0,
        tiled=True,
    ).reshape(slot_total, model_width)
    returned_grads = lax.all_to_all(
        grad_rows.reshape(experts, capacity, model_width),
        "expert",
        split_axis=0,
        concat_axis=0,
        tiled=True,
    ).reshape(slot_total, model_width)
    picked = returned[places]
    weighted = flat_gates[:, None] * picked.astype(jnp.float32)
    mixed_rows = jnp.sum(weighted.reshape(row_count, top_count, model_width), axis=1).astype(
        jnp.bfloat16
    )
    gate_grads = jnp.einsum(
        "jd,jd->j", upstream, picked, preferred_element_type=jnp.float32
    ).reshape(row_count, top_count)
    picked_grads = returned_grads[places].astype(jnp.float32)
    row_grads = jnp.sum(picked_grads.reshape(row_count, top_count, model_width), axis=1).astype(
        jnp.bfloat16
    )
    return (mixed_rows, row_grads, gate_grads)


def solution(mesh):
    return jax.shard_map(
        local,
        mesh=mesh,
        in_specs=(
            P(("dp", "expert"), None),
            P(("dp", "expert"), None),
            P(("dp", "expert"), None),
            P("expert", None, None),
            P("expert", None, None),
            P("expert", None, None),
            P(("dp", "expert"), None),
        ),
        out_specs=(P(("dp", "expert"), None), P(("dp", "expert"), None), P(("dp", "expert"), None)),
        check_vma=False,
    )
```

profile of v0, /device:TPU:32, one launch (start us, length us, event | category | flops | bytes accessed | tf_op | source)
XLA Modules:
  0.0 932.4 jit_solution(493597241722205819)
XLA Ops:
  7.2 0.0 copy-start
  7.2 0.0 copy-start.5
  7.2 0.0 all-gather.7.cloned.1.call-start
  7.2 0.7 all-gather.7.cloned.1.call-update
  7.9 0.0 all-gather.5.cloned.1.call-start
  8.0 0.7 all-gather.5.cloned.1.call-update
  8.7 366.2 %all-gather = s32[128,16,8]{1,2,0:T(8,128)} all-gather(s32[1,16,8]{1,2,0:T(8,128)} %bitcast.48), channel_id=1, replica_groups=mesh['expert'=128,'dp'=2] {'expert'}, dimensions={0}, use_global_device_ids=true | all-gather | bytes 66048 | tf_op jit(solution)/shard_map/all_gather | solution.py:53
  374.9 1.2 copy.23
  376.1 1.4 copy.24
  377.5 1.7 reshape.152
  379.2 0.2 reduce_window_sum.24
  379.4 0.1 copy.25
  379.5 0.0 copy-done.5
  379.5 367.1 %all-gather.1 = f32[128,16,8]{1,2,0:T(8,128)} all-gather(f32[1,16,8]{1,2,0:T(8,128)S(1)} %bitcast.49), channel_id=1, replica_groups=mesh['expert'=128,'dp'=2] {'expert'}, dimensions={0}, use_global_device_ids=true | all-gather | bytes 66048 | tf_op jit(solution)/shard_map/all_gather | solution.py:54
  746.6 2.4 copy.28
  749.0 1.6 reshape.147
  750.6 0.1 add_bitcast_fusion
  750.7 0.1 add.96
  750.8 0.2 compare_select_fusion
  751.0 60.3 %scatter_custom_fusion = s32[257]{0:T(512)S(1)} fusion(s32[16384]{0:T(1024)S(1)} %bitcast.47, s32[16384]{0:T(1024)S(1)} %add_bitcast_fusion, s32[]{:T(128)} %constant.19.clone.1), kind=kCustom, calls=%fused_computation.54 | custom fusion | bytes 1032 | tf_op jit(solution)/shard_map/scatter | solution.py:69
  811.3 1.9 gather_fusion.2
  813.2 0.0 all-gather.7.cloned.1.call-done
  813.3 8.3 concatenate.11
  821.5 7.8 gather_fusion.3
  829.3 8.3 concatenate.9
  837.6 7.9 gather_fusion
  845.5 3.3 fusion.10
  848.8 0.0 copy-done
  848.8 0.0 copy-done.2
  848.8 0.0 copy-start.8
  848.8 0.0 copy-start.1
  848.8 0.0 copy-start.7
  848.8 1.0 fusion.6
  849.8 0.5 copy-done.1
  850.3 1.0 copy-done.7
  851.3 1.0 fusion
  852.3 0.0 copy-start.6
  852.4 1.0 fusion.4
  853.4 0.8 copy-done.6
  854.2 2.3 fusion.15
  856.5 2.5 reshape.148
  859.0 6.4 all-to-all-start.1
  865.5 4.4 fusion.18
  869.9 2.5 reshape.145
  872.4 14.2 %all-to-all-done.1 = bf16[128,2,2048]{2,1,0:T(2,128)(2,1)} async-done(((bf16[128,2,2048]{2,1,0:T(2,128)(2,1)}), bf16[128,2,2048]{2,1,0:T(2,128)(2,1)}, u32[]{:S(2)}, u32[]{:S(2)}) %all-to-all-start.1) | async-done | bytes 1048608 | tf_op jit(solution)/shard_map/all_to_all | solution.py:85
  886.6 7.7 all-to-all-start
  894.3 0.1 copy.27
  894.4 0.1 copy.22
  894.5 0.1 eq.47
  894.5 0.1 fusion.27
  894.6 0.2 reduce_window_sum.26
  894.8 0.1 copy.26
  894.9 0.1 mul.91
  895.0 0.2 select_reduce_fusion
  895.2 2.3 reshape.149
  897.4 3.6 gather_fusion.4
  901.0 2.0 bitcast_reduce_fusion
  903.0 12.6 %all-to-all-done = bf16[128,2,2048]{2,1,0:T(2,128)(2,1)} async-done(((bf16[128,2,2048]{2,1,0:T(2,128)(2,1)}), bf16[128,2,2048]{2,1,0:T(2,128)(2,1)}, u32[]{:S(2)}, u32[]{:S(2)}) %all-to-all-start) | async-done | bytes 1048608 | tf_op jit(solution)/shard_map/all_to_all | solution.py:78
  915.6 2.2 reshape.146
  917.8 3.6 gather_fusion.1
  921.4 1.3 fusion.22
  922.7 2.1 fusion.21
  924.8 0.1 reshape.151
  924.9 0.7 copy.29
  (20 shorter events, 0.1 us)
Async XLA Ops:
  7.2 841.6 %copy-start = (bf16[1,2048,768]{2,1,0:T(8,128)(2,1)S(1)}, bf16[1,2048,768]{2,1,0:T(8,128)(2,1)}, u32[]{:S(2)}) copy-start(bf16[1,2048,768]{2,1,0:T(8,128)(2,1)} %param.11) | copy-start | bytes 9437188
  7.2 372.3 %copy-start.5 = (f32[16,8]{0,1:T(8,128)S(1)}, f32[16,8]{0,1:T(8,128)}, u32[]{:S(2)}) copy-start(f32[16,8]{0,1:T(8,128)} %param.9) | copy-start | bytes 1540
  7.2 806.1 %all-gather.7.cloned.1.call-start = ((), (), s32[]{:S(2)}) async-start(), calls=%async_computation.3 | async-start | bytes 8454144 | tf_op jit(solution)/shard_map/all_gather | solution.py:57
  7.9 821.4 %all-gather.5.cloned.1.call-start = ((), (), s32[]{:S(2)}) async-start(), calls=%async_computation.2 | async-start | bytes 8454144 | tf_op jit(solution)/shard_map/all_gather | solution.py:56
  845.5 3.3 copy-start.2
  848.8 4.6 copy-start.8
  848.8 1.5 copy-start.1
  848.8 2.5 copy-start.7
  851.3 2.1 copy-start.9
  852.3 1.9 copy-start.6
  859.0 27.5 %all-to-all-start.1 = ((bf16[128,2,2048]{2,1,0:T(2,128)(2,1)}), bf16[128,2,2048]{2,1,0:T(2,128)(2,1)}, u32[]{:S(2)}, u32[]{:S(2)}) async-start(bf16[128,2,2048]{2,1,0:T(2,128)(2,1)} %reshape.148), calls=%async_computation.1 | async-start | bytes 2097152 | tf_op jit(solution)/shard_map/all_to_all | solution.py:85
  869.9 24.4 %copy-start.4 = (s32[16,8]{0,1:T(8,128)S(1)}, s32[16,8]{0,1:T(8,128)}, u32[]{:S(2)}) copy-start(s32[16,8]{0,1:T(8,128)} %param.8) | copy-start | bytes 1540
  886.6 29.0 %all-to-all-start = ((bf16[128,2,2048]{2,1,0:T(2,128)(2,1)}), bf16[128,2,2048]{2,1,0:T(2,128)(2,1)}, u32[]{:S(2)}, u32[]{:S(2)}) async-start(bf16[128,2,2048]{2,1,0:T(2,128)(2,1)} %reshape.145), calls=%async_computation | async-start | bytes 2097152 | tf_op jit(solution)/shard_map/all_to_all | solution.py:78
  903.0 18.4 %copy-start.3 = (bf16[16,2048]{1,0:T(8,128)(2,1)S(1)}, bf16[16,2048]{1,0:T(8,128)(2,1)}, u32[]{:S(2)}) copy-start(bf16[16,2048]{1,0:T(8,128)(2,1)} %param.13) | copy-start | bytes 196612
Sparse Core Ops, SparseCore 0:
  11.6 126.3 all-gather.6
  141.6 121.2 all-gather.4
where the time goes:
time: 933 us; the launch traced here: 932 us
  blocking collectives  733 us (79%)
  local copies, waits for them, and re-layouts  123 us (13%)
  waiting for transfers between devices  28.1 us (3%)
  between operations  14.3 us (2%)
  starting transfers between devices  14.2 us (2%)
  matrix products  12.9 us (1%)
    all_gather x1, blocking collectives, local(): all_gates = lax.all_gather(gate_values, 'expert', axis=0, tiled=True)  367 us
    all_gather x1, blocking collectives, local(): gathered_ids = lax.all_gather(expert_ids, 'expert', axis=0, tiled=True)  366 us
    scatter x1, local copies, waits for them, and re-layouts, local(): slot_table = jnp.full((slot_total + 1,), experts * entry_count, jnp.int32...  60.3 us
  transfers between devices with their start and end apart: 4, of which 2 were waited for; matrix products, arithmetic and copies ran while one was open for 11% of the time, Pallas kernels for 0%

commit v1 on v0

--- a/solution.py
+++ b/solution.py
@@ -51,7 +51,9 @@
     upstream = jnp.repeat(cotangent, top_count, axis=0)
     padding = jnp.zeros((1, model_width), jnp.bfloat16)
     gathered_ids = lax.all_gather(expert_ids, "expert", axis=0, tiled=True)
-    all_gates = lax.all_gather(gate_values, "expert", axis=0, tiled=True)
+    all_gates = jnp.concatenate(
+        lax.all_to_all(jnp.stack([gate_values] * lax.axis_size("expert")), "expert", 0, 0), axis=0
+    )
     all_tokens, all_cotangent = (
         lax.all_gather(tokens, "expert", axis=0, tiled=True),
         lax.all_gather(cotangent, "expert", axis=0, tiled=True),

time: 933 us -> 591 us (0.63)
  blocking collectives: 733 us -> 364 us
  starting transfers between devices: 14.2 us -> 35.3 us
    all_gather x1 -> x0, blocking collectives: 367 us -> none  [local(): all_gates = lax.all_gather(gate_values, 'expert', axis=0, tiled=True)]
    all_to_all x0 -> x1, starting transfers between devices: none -> 15 us  [local(): lax.all_to_all(jnp.stack([gate_values] * lax.axis_size('expert')), 'exper...]
  transfers between devices with their start and end apart: 4 -> 5, of which waited for: 2 -> 2; matrix products, arithmetic and copies ran while one was open for 11% -> 18% of each run, Pallas kernels for 0% -> 0%
where the time goes in v1:
time: 591 us; the launch traced here: 590 us
  blocking collectives  364 us (62%)
  local copies, waits for them, and re-layouts  128 us (22%)
  starting transfers between devices  35.3 us (6%)
  waiting for transfers between devices  28.3 us (5%)
  between operations  14.4 us (2%)
  matrix products  12.9 us (2%)
  other arithmetic  7.13 us (1%)
    all_gather x1, blocking collectives, local(): gathered_ids = lax.all_gather(expert_ids, 'expert', axis=0, tiled=True)  364 us
    scatter x1, local copies, waits for them, and re-layouts, local(): slot_table = jnp.full((slot_total + 1,), experts * entry_count, jnp.int32...  60.3 us
    all_to_all x1, starting transfers between devices, local(): lax.all_to_all(jnp.stack([gate_values] * lax.axis_size('expert')), 'exper...  15 us
    all_to_all x1, waiting for transfers between devices, local(): lax.all_to_all(grad_rows.reshape(experts, capacity, model_width), 'expert...  14.3 us
    all_to_all x1, waiting for transfers between devices, local(): lax.all_to_all(output.reshape(experts, capacity, model_width), 'expert',...  12.5 us
    all_to_all x1, starting transfers between devices, local(): lax.all_to_all(grad_rows.reshape(experts, capacity, model_width), 'expert...  12.5 us
  transfers between devices with their start and end apart: 5, of which 2 were waited for; matrix products, arithmetic and copies ran while one was open for 18% of the time, Pallas kernels for 0%

profile of v1, /device:TPU:32, one launch (start us, length us, event | category | flops | bytes accessed | tf_op | source)
XLA Modules:
  0.0 590.4 jit_solution(17307392358107242303)
XLA Ops:
  7.2 0.0 copy-start
  7.2 0.0 all-gather.6.cloned.1.call-start
  7.2 0.7 all-gather.6.cloned.1.call-update
  7.9 0.0 all-gather.4.cloned.1.call-start
  8.0 0.7 all-gather.4.cloned.1.call-update
  8.7 1.5 broadcast_bitcast_fusion
  10.2 1.9 reshape.216
  12.1 15.0 %all-to-all-start.1 = ((f32[128,1,128]{2,1,0:T(1,128)}), f32[128,1,128]{2,1,0:T(1,128)S(1)}, u32[]{:S(2)}, u32[]{:S(2)}) async-start(f32[128,1,128]{2,1,0:T(1,128)} %reshape.216), calls=%async_computation.1 | async-start | bytes 131072 | tf_op jit(solution)/shard_map/all_to_all | solution.py:55
  27.1 364.2 %all-gather = s32[128,16,8]{1,2,0:T(8,128)} all-gather(s32[1,16,8]{1,2,0:T(8,128)} %bitcast.51), channel_id=1, replica_groups=mesh['expert'=128,'dp'=2] {'expert'}, dimensions={0}, use_global_device_ids=true | all-gather | bytes 66048 | tf_op jit(solution)/shard_map/all_gather | solution.py:53
  391.2 1.2 copy.24
  392.5 1.4 copy.25
  393.8 1.7 reshape.150
  395.6 0.2 reduce_window_sum.24
  395.8 0.1 copy.26
  395.9 0.1 add_bitcast_fusion
  396.0 0.1 add.96
  396.0 0.2 compare_select_fusion
  396.2 60.3 %scatter_custom_fusion = s32[257]{0:T(512)S(1)} fusion(s32[16384]{0:T(1024)S(1)} %bitcast.50, s32[16384]{0:T(1024)S(1)} %add_bitcast_fusion, s32[]{:T(128)} %constant.19.clone.1), kind=kCustom, calls=%fused_computation.54 | custom fusion | bytes 1032 | tf_op jit(solution)/shard_map/scatter | solution.py:71
  456.5 0.0 all-to-all-done.1
  456.6 0.5 broadcast.160
  457.1 0.8 reduce.3
  457.9 1.0 reshape.217
  458.9 2.4 copy.29
  461.3 1.6 reshape_reshape.3
  462.9 1.9 gather_fusion.2
  464.9 0.0 all-gather.6.cloned.1.call-done
  464.9 8.3 %concatenate.11 = bf16[2049,2048]{1,0:T(8,128)(2,1)} pad(bf16[2048,2048]{1,0:T(8,128)(2,1)} %all-gather.6.cloned.1.call-done, bf16[]{:T(256)} %constant.18.clone.1), padding=0_1x0_0 | pad | bytes 16781314 | tf_op jit(solution)/shard_map/concatenate | solution.py:77
  473.2 7.8 %gather_fusion.3 = bf16[256,2048]{1,0:T(8,128)(2,1)} fusion(bf16[2049,2048]{1,0:T(8,128)(2,1)} %concatenate.11, s32[1024]{0:T(1024)S(1)} %pad_clamp_fusion.2), kind=kCustom, calls=%fused_computation.3 | custom fusion | bytes 2098176 | tf_op jit(solution)/shard_map/gather | solution.py:77
  481.0 8.3 %concatenate.9 = bf16[2049,2048]{1,0:T(8,128)(2,1)} pad(bf16[2048,2048]{1,0:T(8,128)(2,1)} %all-gather.4.cloned.1.call-done, bf16[]{:T(256)} %constant.18.clone.1), padding=0_1x0_0 | pad | bytes 16781314 | tf_op jit(solution)/shard_map/concatenate | solution.py:74
  489.3 7.9 %gather_fusion = bf16[256,2048]{1,0:T(8,128)(2,1)} fusion(bf16[2049,2048]{1,0:T(8,128)(2,1)} %concatenate.9, s32[1024]{0:T(1024)S(1)} %pad_clamp_fusion.2), kind=kCustom, calls=%fused_computation | custom fusion | bytes 2098176 | tf_op jit(solution)/shard_map/gather | solution.py:74
  497.2 3.3 fusion.10
  500.5 0.0 copy-start.7
  500.5 1.0 fusion.6
  501.5 0.5 copy-done.1
  502.0 1.0 copy-done.7
  502.9 1.0 fusion
  504.0 0.0 copy-start.6
  504.0 1.0 fusion.4
  505.0 0.8 copy-done.6
  505.9 2.3 fusion.15
  508.2 2.5 reshape.146
  510.7 12.5 %all-to-all-start.2 = ((bf16[128,2,2048]{2,1,0:T(2,128)(2,1)}), bf16[128,2,2048]{2,1,0:T(2,128)(2,1)}, u32[]{:S(2)}, u32[]{:S(2)}) async-start(bf16[128,2,2048]{2,1,0:T(2,128)(2,1)} %reshape.146), calls=%async_computation.2 | async-start | bytes 2097152 | tf_op jit(solution)/shard_map/all_to_all | solution.py:87
  523.2 4.4 fusion.18
  527.6 2.6 reshape.144
  530.2 14.3 %all-to-all-done.2 = bf16[128,2,2048]{2,1,0:T(2,128)(2,1)} async-done(((bf16[128,2,2048]{2,1,0:T(2,128)(2,1)}), bf16[128,2,2048]{2,1,0:T(2,128)(2,1)}, u32[]{:S(2)}, u32[]{:S(2)}) %all-to-all-start.2) | async-done | bytes 1048608 | tf_op jit(solution)/shard_map/all_to_all | solution.py:87
  544.5 7.7 %all-to-all-start = ((bf16[128,2,2048]{2,1,0:T(2,128)(2,1)}), bf16[128,2,2048]{2,1,0:T(2,128)(2,1)}, u32[]{:S(2)}, u32[]{:S(2)}) async-start(bf16[128,2,2048]{2,1,0:T(2,128)(2,1)} %reshape.144), calls=%async_computation | async-start | bytes 2097152 | tf_op jit(solution)/shard_map/all_to_all | solution.py:80
  552.2 0.1 copy.28
  552.3 0.1 copy.23
  552.4 0.1 eq.47
  552.4 0.1 fusion.27
  552.5 0.2 reduce_window_sum.26
  552.7 0.1 copy.27
  552.8 0.1 mul.91
  552.9 0.2 select_reduce_fusion
  553.1 2.3 reshape.147
  555.3 3.6 gather_fusion.4
  558.9 2.0 bitcast_reduce_fusion
  561.0 12.5 %all-to-all-done = bf16[128,2,2048]{2,1,0:T(2,128)(2,1)} async-done(((bf16[128,2,2048]{2,1,0:T(2,128)(2,1)}), bf16[128,2,2048]{2,1,0:T(2,128)(2,1)}, u32[]{:S(2)}, u32[]{:S(2)}) %all-to-all-start) | async-done | bytes 1048608 | tf_op jit(solution)/shard_map/all_to_all | solution.py:80
  573.5 2.3 reshape.145
  575.8 3.6 gather_fusion.1
  579.4 1.3 fusion.22
  580.6 2.1 fusion.21
  582.8 0.1 reshape.149
  582.8 0.7 copy.30
  (26 shorter events, 0.1 us)
Async XLA Ops:
  7.2 493.3 %copy-start = (bf16[1,2048,768]{2,1,0:T(8,128)(2,1)S(1)}, bf16[1,2048,768]{2,1,0:T(8,128)(2,1)}, u32[]{:S(2)}) copy-start(bf16[1,2048,768]{2,1,0:T(8,128)(2,1)} %param.11) | copy-start | bytes 9437188
  7.2 457.7 %all-gather.6.cloned.1.call-start = ((), (), s32[]{:S(2)}) async-start(), calls=%async_computation.4 | async-start | bytes 8454144 | tf_op jit(solution)/shard_map/all_gather | solution.py:59
  7.9 473.1 %all-gather.4.cloned.1.call-start = ((), (), s32[]{:S(2)}) async-start(), calls=%async_computation.3 | async-start | bytes 8454144 | tf_op jit(solution)/shard_map/all_gather | solution.py:58
  12.1 444.5 %all-to-all-start.1 = ((f32[128,1,128]{2,1,0:T(1,128)}), f32[128,1,128]{2,1,0:T(1,128)S(1)}, u32[]{:S(2)}, u32[]{:S(2)}) async-start(f32[128,1,128]{2,1,0:T(1,128)} %reshape.216), calls=%async_computation.1 | async-start | bytes 131072 | tf_op jit(solution)/shard_map/all_to_all | solution.py:55
  497.2 3.3 copy-start.2
  500.4 4.6 copy-start.8
  500.5 1.5 copy-start.1
  500.5 2.5 copy-start.7
  502.9 2.1 copy-start.9
  504.0 1.9 copy-start.6
  510.7 33.8 %all-to-all-start.2 = ((bf16[128,2,2048]{2,1,0:T(2,128)(2,1)}), bf16[128,2,2048]{2,1,0:T(2,128)(2,1)}, u32[]{:S(2)}, u32[]{:S(2)}) async-start(bf16[128,2,2048]{2,1,0:T(2,128)(2,1)} %reshape.146), calls=%async_computation.2 | async-start | bytes 2097152 | tf_op jit(solution)/shard_map/all_to_all | solution.py:87
  527.6 24.6 %copy-start.4 = (s32[16,8]{0,1:T(8,128)S(1)}, s32[16,8]{0,1:T(8,128)}, u32[]{:S(2)}) copy-start(s32[16,8]{0,1:T(8,128)} %param.8) | copy-start | bytes 1540
  527.6 24.7 %copy-start.5 = (f32[16,8]{0,1:T(8,128)S(1)}, f32[16,8]{0,1:T(8,128)}, u32[]{:S(2)}) copy-start(f32[16,8]{0,1:T(8,128)} %param.9) | copy-start | bytes 1540
  544.5 29.0 %all-to-all-start = ((bf16[128,2,2048]{2,1,0:T(2,128)(2,1)}), bf16[128,2,2048]{2,1,0:T(2,128)(2,1)}, u32[]{:S(2)}, u32[]{:S(2)}) async-start(bf16[128,2,2048]{2,1,0:T(2,128)(2,1)} %reshape.144), calls=%async_computation | async-start | bytes 2097152 | tf_op jit(solution)/shard_map/all_to_all | solution.py:80
  561.0 18.4 %copy-start.3 = (bf16[16,2048]{1,0:T(8,128)(2,1)S(1)}, bf16[16,2048]{1,0:T(8,128)(2,1)}, u32[]{:S(2)}) copy-start(bf16[16,2048]{1,0:T(8,128)(2,1)} %param.13) | copy-start | bytes 196612
Sparse Core Ops, SparseCore 0:
  11.6 126.3 all-gather.5
  141.6 121.1 all-gather.3
